TPU v7x, 512 devices: a whole 4x8x8 slice. The times are simulated.
512 devices in a mesh: expert: 16 (over z, core), tensor: 32 (over x, y).
Axes of the slice: x: 4, y: 8, z: 8, core: 2. Of those that a mesh axis runs over, the one named last changes fastest.
Arguments:
- tokens: bfloat16 [2048, 5120], P('expert', 'tensor'), may hold values from -6 to 6
- routes: int32 [2048, 6], P('expert'), may hold values from 0 to 15, all different within a row; in each aligned block of 128 rows (0 to 127, 128 to 255, ...) at most 64 rows name the same one
- gates: float32 [2048, 6], P('expert'), may hold values from 0.05 to 0.35
- w_gate: bfloat16 [16, 1536, 5120], P('expert', 'tensor'), may hold values from -0.078125 to 0.078125
- w_up: bfloat16 [16, 1536, 5120], P('expert', 'tensor'), may hold values from -0.078125 to 0.078125
- w_down: bfloat16 [16, 1536, 5120], P('expert', None, 'tensor'), may hold values from -0.15625 to 0.15625
- shared_gate: bfloat16 [1536, 5120], P('tensor'), may hold values from -0.078125 to 0.078125
- shared_up: bfloat16 [1536, 5120], P('tensor'), may hold values from -0.078125 to 0.078125
- shared_down: bfloat16 [1536, 5120], P(None, 'tensor'), may hold values from -0.15625 to 0.15625
- vocab: bfloat16 [65536, 5120], P(('expert', 'tensor'))
- targets: int32 [64], replicated, may hold values from 0 to 65535
Outputs:
- layer_out: bfloat16 [2048, 5120], P('expert', 'tensor')
- loglik: float32 [64], replicated
Inputs may be any that keep to these rules, and one draw needn't show every extreme that they name: `routes`: the tokens of one group name one expert at most 64 times; in every draw some group names some expert exactly 64 times.
All inputs are finite; a program needn't handle non-finite values.
Results may differ from a plain program's by a relative error of at most 0.0041.
Values may be sent and summed in bfloat16 or wider, within the bound.
No kernel may reach another device: no remote copies, remote signals or barrier semaphores. Data moves between devices by JAX's collectives and lax.ppermute only.
A program may use at most 64 MiB of HBM per device.

v0:
```python
import jax
import jax.numpy as jnp
from jax import lax
from jax.sharding import PartitionSpec as P

EXPERTS = 16
SCORE_E = 4


def slot_tables(routes, gates, capacity):
    picks = (routes[:, :, None] == jnp.arange(EXPERTS, dtype=jnp.int32)[None, None, :]).astype(
        jnp.int32
    )
    per_token = jnp.sum(picks, axis=1)
    earlier = jnp.cumsum(per_token, axis=0) - per_token
    slots = jnp.sum(picks * earlier[:, None, :], axis=2)
    places = (slots[:, :, None] == jnp.arange(capacity, dtype=jnp.int32)[None, None, :]).astype(
        jnp.float32
    )
    picked = picks.astype(jnp.float32)
    select = jnp.einsum("ikr,iks->rsi", picked, places, precision=lax.Precision.HIGHEST)
    weigh = jnp.einsum("ikr,iks,ik->rsi", picked, places, gates, precision=lax.Precision.HIGHEST)
    return (select.astype(jnp.bfloat16), weigh)


def contract_last(left, right):
    return lax.dot_general(
        left, right, (((1,), (1,)), ((), ())), preferred_element_type=jnp.float32
    )


def shards(
    tokens, routes, gates, w_gate, w_up, w_down, shared_gate, shared_up, shared_down, vocab, targets
):
    tok_rows = tokens.shape[0]
    capacity = tok_rows // 2
    groups = lax.axis_size("expert")
    lanes = lax.axis_size("tensor")
    exp_dev = w_gate.shape[0]
    width = w_gate.shape[1]
    out_width = w_down.shape[2]
    select, weigh = slot_tables(routes, gates, capacity)
    outgoing = jnp.einsum("rsi,id->rsd", select, tokens, preferred_element_type=jnp.float32).astype(
        jnp.bfloat16
    )
    arrived = lax.all_to_all(outgoing, "expert", split_axis=0, concat_axis=1, tiled=True)
    slot_count = arrived.shape[1]
    flat_rows = arrived.reshape(exp_dev * slot_count, arrived.shape[2])
    pieces = (
        lax.all_gather(flat_rows, "tensor", axis=1, tiled=True),
        lax.all_gather(tokens, "tensor", axis=1, tiled=True),
    )
    span = pieces[0].shape[1]
    rows = pieces[0].reshape(exp_dev, slot_count, span)
    gate_acc = jnp.einsum("erw,efw->erf", rows, w_gate, preferred_element_type=jnp.float32)
    up_acc = jnp.einsum("erw,efw->erf", rows, w_up, preferred_element_type=jnp.float32)
    shared_gate_acc = contract_last(pieces[1], shared_gate)
    shared_up_acc = contract_last(pieces[1], shared_up)
    hidden_routed = (jax.nn.silu(gate_acc) * up_acc).astype(jnp.bfloat16)
    hidden_shared = (jax.nn.silu(shared_gate_acc) * shared_up_acc).astype(jnp.bfloat16)
    flat_hidden = hidden_routed.reshape(exp_dev * slot_count, width)
    pieces = (
        lax.all_gather(flat_hidden, "tensor", axis=1, tiled=True),
        lax.all_gather(hidden_shared, "tensor", axis=1, tiled=True),
    )
    span = pieces[0].shape[1]
    rows = pieces[0].reshape(exp_dev, slot_count, span)
    routed_out = jnp.einsum("erw,ewd->erd", rows, w_down, preferred_element_type=jnp.float32)
    shared_out = jnp.dot(pieces[1], shared_down, preferred_element_type=jnp.float32)
    returned = lax.all_to_all(
        routed_out.astype(jnp.bfloat16), "expert", split_axis=1, concat_axis=0, tiled=True
    )
    routed = jnp.einsum(
        "rsi,rsd->id", weigh, returned.astype(jnp.float32), precision=lax.Precision.HIGHEST
    )
    layer_out = (tokens.astype(jnp.float32) + shared_out + routed).astype(jnp.bfloat16)
    scored = layer_out[tok_rows - SCORE_E :].reshape(1, SCORE_E * out_width)
    collected = lax.all_gather(scored, ("expert", "tensor"), axis=0, tiled=True)
    full_rows = (
        collected.reshape(groups, lanes, SCORE_E, out_width)
        .transpose(0, 2, 1, 3)
        .reshape(groups * SCORE_E, lanes * out_width)
    )
    logits = contract_last(full_rows, vocab)
    exp_sums = jnp.sum(jnp.exp(logits), axis=1)
    offset = (lax.axis_index("expert") * lanes + lax.axis_index("tensor")) * vocab.shape[0]
    columns = offset + jnp.arange(vocab.shape[0], dtype=jnp.int32)
    target_part = jnp.sum(jnp.where(targets[:, None] == columns[None, :], logits, 0.0), axis=1)
    totals, target_logit = lax.psum((exp_sums, target_part), ("expert", "tensor"))
    loglik = target_logit - jnp.log(totals)
    return (layer_out, loglik)


def solution(mesh):
    placed = (
        P("expert", "tensor"),
        P("expert", None),
        P("expert", None),
        P("expert", "tensor", None),
        P("expert", "tensor", None),
        P("expert", None, "tensor"),
        P("tensor", None),
        P("tensor", None),
        P(None, "tensor"),
        P(("expert", "tensor"), None),
        P(),
    )
    return jax.shard_map(
        shards, mesh=mesh, in_specs=placed, out_specs=(P("expert", "tensor"), P()), check_vma=False
    )
```

profile of v0, /device:TPU:1, one launch (start us, length us, event | category | flops | bytes accessed | tf_op | source)
XLA Modules:
  0.0 622.9 jit_solution(7036797286087049021)
XLA Ops:
  7.2 0.9 copy.21
  8.6 2.4 select_reduce_fusion
  11.0 1.2 fusion
  12.6 29.1 %all_to_all.21 = bf16[16,64,160]{2,1,0:T(8,128)(2,1)S(1)} all-to-all(bf16[16,64,160]{2,1,0:T(8,128)(2,1)S(1)} %convolution_convert_fusion.1), channel_id=1, replica_groups=mesh['expert'=16,'tensor'=32] {'expert'}, dimensions={0} | all-to-all | bytes 655360 | tf_op jit(solution)/shard_map/all_to_all | solution.py:46
  41.7 0.9 copy.24
  42.7 110.4 %all-gather.7.cloned.1.call-done = bf16[1024,5120]{0,1:T(8,128)(2,1)} async-done(((bf16[1024,160]{0,1:T(8,128)(2,1)}), bf16[1024,5120]{0,1:T(8,128)(2,1)}) %all-gather.7.cloned.1.call-update) | async-done | bytes 10485776 | tf_op jit(solution)/shard_map/all_gather | solution.py:50
  153.1 6.1 fusion.11
  159.2 0.9 copy-done.1
  160.0 2.6 fusion.2
  162.9 0.5 all-gather.5.cloned.1.call-update
  163.6 2.7 convolution_bitcast_fusion
  166.3 76.0 %all-gather.9.cloned.1.call-done = bf16[1024,1536]{0,1:T(8,128)(2,1)} async-done(((bf16[1024,48]{0,1:T(8,128)(2,1)}), bf16[1024,1536]{0,1:T(8,128)(2,1)}) %all-gather.9.cloned.1.call-update) | async-done | bytes 3145744 | tf_op jit(solution)/shard_map/all_gather | solution.py:63
  242.3 2.6 fusion.1
  244.9 0.8 copy.25
  245.8 0.5 broadcast.28
  246.3 4.0 reduce.1
  250.3 1.5 reshape.84
  251.8 11.8 %all-to-all-start.1 = ((bf16[16,2,5120]{2,1,0:T(2,128)(2,1)}), bf16[16,2,5120]{2,1,0:T(2,128)(2,1)S(1)}, u32[]{:S(2)}, u32[]{:S(2)}) async-start(bf16[16,2,5120]{2,1,0:T(2,128)(2,1)} %reshape.84), calls=%async_computation.1 | async-start | bytes 655360 | tf_op jit(solution)/shard_map/all_to_all | solution.py:70
  263.6 60.0 %all-gather.5.cloned.1.call-done = bf16[128,5120]{0,1:T(8,128)(2,1)} async-done(((bf16[128,160]{0,1:T(8,128)(2,1)}), bf16[128,5120]{0,1:T(8,128)(2,1)}) %all-gather.5.cloned.1.call-update) | async-done | bytes 1310736 | tf_op jit(solution)/shard_map/all_gather | solution.py:51
  323.6 1.8 fusion.21
  325.3 0.4 fusion.5
  325.7 36.5 %all_gather.16 = bf16[128,1536]{0,1:T(8,128)(2,1)S(1)} all-gather(bf16[128,48]{0,1:T(8,128)(2,1)S(1)} %fusion.5), channel_id=1, replica_groups=mesh['expert'=16,'tensor'=32] {'tensor'}, dimensions={1}, use_global_device_ids=true | all-gather | bytes 405504 | tf_op jit(solution)/shard_map/all_gather | solution.py:64
  362.2 0.9 reshape.85
  363.2 1.1 copy-done.5
  364.3 1.1 convolution_bitcast_fusion.1
  366.1 145.7 %all-gather = bf16[512,1,640]{2,1,0:T(2,128)(2,1)S(1)} all-gather(bf16[1,1,640]{2,1,0:T(2,128)(2,1)S(1)} %reshape.76), channel_id=1, replica_groups=mesh['expert'=16,'tensor'=32] {'expert','tensor'}, dimensions={0}, use_global_device_ids=true | all-gather | bytes 656640 | tf_op jit(solution)/shard_map/all_gather | solution.py:78
  511.8 4.0 reduce
  515.8 0.7 reshape.74
  516.7 1.7 reshape.75
  518.4 0.7 exponential_reduce_fusion
  519.1 96.8 %all-reduce = (f32[64]{0:T(128)S(1)}, f32[64]{0:T(128)S(1)}) all-reduce(f32[64]{0:T(128)S(1)} %get-tuple-element.3, f32[64]{0:T(128)S(1)} %get-tuple-element.2), channel_id=1, replica_groups=mesh['expert'=16,'tensor'=32] {'expert','tensor'}, use_global_device_ids=true, to_apply=%region_4.5 | all-reduce | flops 128 | bytes 1024 | tf_op jit(solution)/shard_map/psum | solution.py:89
  615.9 0.5 log_subtract_fusion
  (46 shorter events, 2.1 us)
Async XLA Ops:
  7.2 511.2 %copy-start = (bf16[128,5120]{1,0:T(8,128)(2,1)S(1)}, bf16[128,5120]{1,0:T(8,128)(2,1)}, u32[]{:S(2)}) copy-start(bf16[128,5120]{1,0:T(8,128)(2,1)} %param.20) | copy-start | bytes 3932164
  7.2 145.9 %all-gather.7.cloned.1.call-start = ((), (), s32[]{:S(2)}) async-start(), calls=%async_computation.3 | async-start | bytes 10813440 | tf_op jit(solution)/shard_map/all_gather | solution.py:50
  8.4 3.8 copy-start.10
  12.6 140.5 %copy-start.3 = (bf16[1,48,5120]{2,1,0:T(8,128)(2,1)S(1)}, bf16[1,48,5120]{2,1,0:T(8,128)(2,1)}, u32[]{:S(2)}) copy-start(bf16[1,48,5120]{2,1,0:T(8,128)(2,1)} %param.14) | copy-start | bytes 1474564
  42.6 116.5 %copy-start.4 = (bf16[1,48,5120]{2,1,0:T(8,128)(2,1)S(1)}, bf16[1,48,5120]{2,1,0:T(8,128)(2,1)}, u32[]{:S(2)}) copy-start(bf16[1,48,5120]{2,1,0:T(8,128)(2,1)} %param.15) | copy-start | bytes 1474564
  42.6 199.7 %all-gather.9.cloned.1.call-start = ((), (), s32[]{:S(2)}) async-start(), calls=%async_computation.4 | async-start | bytes 3244032 | tf_op jit(solution)/shard_map/all_gather | solution.py:63
  153.1 7.0 %copy-start.1 = (bf16[1024,5120]{0,1:T(8,128)(2,1)S(1)}, bf16[1024,5120]{0,1:T(8,128)(2,1)}, u32[]{:S(2)}) copy-start(bf16[1024,5120]{0,1:T(8,128)(2,1)} %all-gather.7.cloned.1.call-done) | copy-start | bytes 31457284
  160.0 3.4 copy-start.13
  162.7 160.8 %all-gather.5.cloned.1.call-start = ((), (), s32[]{:S(2)}) async-start(), calls=%async_computation.2 | async-start | bytes 1351680 | tf_op jit(solution)/shard_map/all_gather | solution.py:51
  163.6 78.8 %copy-start.8 = (bf16[1,1536,160]{1,2,0:T(8,128)(2,1)S(1)}, bf16[1,1536,160]{1,2,0:T(8,128)(2,1)}, u32[]{:S(2)}) copy-start(bf16[1,1536,160]{1,2,0:T(8,128)(2,1)} %param.16) | copy-start | bytes 1474564
  250.3 73.2 %copy-start.6 = (bf16[48,5120]{1,0:T(8,128)(2,1)S(1)}, bf16[48,5120]{1,0:T(8,128)(2,1)}, u32[]{:S(2)}) copy-start(bf16[48,5120]{1,0:T(8,128)(2,1)} %param.17) | copy-start | bytes 1474564
  251.8 73.5 %copy-start.7 = (bf16[48,5120]{1,0:T(8,128)(2,1)S(1)}, bf16[48,5120]{1,0:T(8,128)(2,1)}, u32[]{:S(2)}) copy-start(bf16[48,5120]{1,0:T(8,128)(2,1)} %param.18) | copy-start | bytes 1474564
  251.8 110.4 %all-to-all-start.1 = ((bf16[16,2,5120]{2,1,0:T(2,128)(2,1)}), bf16[16,2,5120]{2,1,0:T(2,128)(2,1)S(1)}, u32[]{:S(2)}, u32[]{:S(2)}) async-start(bf16[16,2,5120]{2,1,0:T(2,128)(2,1)} %reshape.84), calls=%async_computation.1 | async-start | bytes 655360 | tf_op jit(solution)/shard_map/all_to_all | solution.py:70
  323.6 1.8 copy-start.2
  363.1 1.2 copy-start.5
  363.1 2.4 copy-start.9
  363.1 2.4 copy-start.11
  365.8 150.0 %copy-start.12 = (bf16[128,160]{0,1:T(8,128)(2,1)}, bf16[128,160]{0,1:T(8,128)(2,1)S(1)}, u32[]{:S(2)}) copy-start(bf16[128,160]{0,1:T(8,128)(2,1)S(1)} %fusion.4) | copy-start | bytes 122884
  516.7 1.7 copy-start.14
Sparse Core Ops, SparseCore 0:
  42.7 110.3 all-gather.6
  162.8 79.4 all-gather.8
  245.5 78.0 all-gather.4
where the time goes:
time: 623 us
  blocking collectives  308 us (49%)
  waiting for transfers between devices  247 us (40%)
  matrix products  19.8 us (3%)
  between operations  14.1 us (2%)
  starting transfers between devices  12.1 us (2%)
  other arithmetic  11.4 us (2%)
  local copies, waits for them, and re-layouts  10.7 us (2%)
    all_gather x1, blocking collectives, shards(): collected = lax.all_gather(scored, ('expert', 'tensor'), axis=0, tiled=True)  146 us
    all_gather x1, waiting for transfers between devices, shards(): lax.all_gather(flat_rows, 'tensor', axis=1, tiled=True)  110 us
    psum x1, blocking collectives, shards(): lax.psum((exp_sums, target_part), ('expert', 'tensor'))  96.8 us
    all_gather x1, waiting for transfers between devices, shards(): lax.all_gather(flat_hidden, 'tensor', axis=1, tiled=True)  76 us
    all_gather x1, waiting for transfers between devices, shards(): lax.all_gather(tokens, 'tensor', axis=1, tiled=True)  60 us
    all_gather x1, blocking collectives, shards(): lax.all_gather(hidden_shared, 'tensor', axis=1, tiled=True)  36.5 us
    all_to_all x1, blocking collectives, shards(): lax.all_to_all(outgoing, 'expert', split_axis=0, concat_axis=1, tiled=True)  29.1 us
  transfers between devices with their start and end apart: 4, of which 3 were waited for; matrix products, arithmetic and copies ran while one was open for 2% of the time, Pallas kernels for 0%

commit v1 on v0

--- a/solution.py
+++ b/solution.py
@@ -59,9 +59,22 @@
     hidden_routed = (jax.nn.silu(gate_acc) * up_acc).astype(jnp.bfloat16)
     hidden_shared = (jax.nn.silu(shared_gate_acc) * shared_up_acc).astype(jnp.bfloat16)
     flat_hidden = hidden_routed.reshape(exp_dev * slot_count, width)
+
+    def number_the_core(local_x, join_dim=1):
+        k_all = lax.axis_size("tensor")
+        j = 0
+        nodes = []
+        while j < local_x.ndim:
+            nodes.append(k_all if j == join_dim else 1)
+            j = j + 1
+        piece_now = jnp.tile(local_x, nodes)
+        return lax.all_to_all(
+            piece_now, axis_name="tensor", split_axis=join_dim, concat_axis=join_dim, tiled=True
+        )
+
     pieces = (
         lax.all_gather(flat_hidden, "tensor", axis=1, tiled=True),
-        lax.all_gather(hidden_shared, "tensor", axis=1, tiled=True),
+        number_the_core(hidden_shared),
     )
     span = pieces[0].shape[1]
     rows = pieces[0].reshape(exp_dev, slot_count, span)

time: 623 us -> 591 us (0.949)
  blocking collectives: 308 us -> 262 us
  waiting for transfers between devices: 247 us -> 254 us
    all_gather x1 -> x0, blocking collectives: 36.5 us -> none  [shards(): lax.all_gather(hidden_shared, 'tensor', axis=1, tiled=True)]
    all_gather x1, blocking collectives: 146 us -> 136 us  [shards(): collected = lax.all_gather(scored, ('expert', 'tensor'), axis=0, tiled=True)]
  transfers between devices with their start and end apart: 4 -> 5, of which waited for: 3 -> 4; matrix products, arithmetic and copies ran while one was open for 2% -> 3% of each run, Pallas kernels for 0% -> 0%
where the time goes in v1:
time: 591 us; the launch traced here: 590 us
  blocking collectives  262 us (44%)
  waiting for transfers between devices  254 us (43%)
  matrix products  19.8 us (3%)
  starting transfers between devices  18 us (3%)
  between operations  14.1 us (2%)
  local copies, waits for them, and re-layouts  11.5 us (2%)
  other arithmetic  11.4 us (2%)
    all_gather x1, blocking collectives, shards(): collected = lax.all_gather(scored, ('expert', 'tensor'), axis=0, tiled=True)  136 us
    all_gather x1, waiting for transfers between devices, shards(): lax.all_gather(flat_rows, 'tensor', axis=1, tiled=True)  110 us
    psum x1, blocking collectives, shards(): lax.psum((exp_sums, target_part), ('expert', 'tensor'))  96.8 us
    all_gather x1, waiting for transfers between devices, shards(): lax.all_gather(flat_hidden, 'tensor', axis=1, tiled=True)  78.9 us
    all_gather x1, waiting for transfers between devices, shards(): lax.all_gather(tokens, 'tensor', axis=1, tiled=True)  59.9 us
    all_to_all x1, blocking collectives, shards(): lax.all_to_all(outgoing, 'expert', split_axis=0, concat_axis=1, tiled=True)  29.1 us
  transfers between devices with their start and end apart: 5, of which 4 were waited for; matrix products, arithmetic and copies ran while one was open for 3% of the time, Pallas kernels for 0%

profile of v1, /device:TPU:1, one launch (start us, length us, event | category | flops | bytes accessed | tf_op | source)
XLA Modules:
  0.0 590.4 jit_solution(9935480038216036610)
XLA Ops:
  7.2 0.9 copy.22
  8.6 2.4 select_reduce_fusion
  11.0 1.2 fusion
  12.6 29.1 %all_to_all.30 = bf16[16,64,160]{2,1,0:T(8,128)(2,1)S(1)} all-to-all(bf16[16,64,160]{2,1,0:T(8,128)(2,1)S(1)} %convolution_convert_fusion.1), channel_id=1, replica_groups=mesh['expert'=16,'tensor'=32] {'expert'}, dimensions={0} | all-to-all | bytes 655360 | tf_op jit(solution)/shard_map/all_to_all | solution.py:46
  41.7 0.9 copy.25
  42.7 110.4 %all-gather.7.cloned.1.call-done = bf16[1024,5120]{0,1:T(8,128)(2,1)} async-done(((bf16[1024,160]{0,1:T(8,128)(2,1)}), bf16[1024,5120]{0,1:T(8,128)(2,1)}) %all-gather.7.cloned.1.call-update) | async-done | bytes 10485776 | tf_op jit(solution)/shard_map/all_gather | solution.py:50
  153.1 6.1 %fusion.11 = f32[1024,48]{0,1:T(8,128)S(1)} fusion(bf16[1024,5120]{0,1:T(8,128)(2,1)} %all-gather.7.cloned.1.call-done, bf16[1,48,5120]{2,1,0:T(8,128)(2,1)S(1)} %copy-done.3), kind=kOutput, calls=%fused_computation.24 | convolution fusion | flops 503316480 | bytes 11173888 | tf_op jit(solution)/shard_map/erw,efw->erf/dot_general | solution.py:55
  159.2 0.9 copy-done.1
  160.0 2.6 fusion.2
  163.4 78.9 %all-gather.9.cloned.1.call-done = bf16[1024,1536]{0,1:T(8,128)(2,1)} async-done(((bf16[1024,48]{0,1:T(8,128)(2,1)}), bf16[1024,1536]{0,1:T(8,128)(2,1)}) %all-gather.9.cloned.1.call-update) | async-done | bytes 3145744 | tf_op jit(solution)/shard_map/all_gather | solution.py:76
  242.3 2.6 fusion.1
  244.9 0.8 copy.26
  245.8 0.5 broadcast.31
  246.3 4.0 reduce.1
  250.3 1.5 reshape.91
  251.9 11.8 %all-to-all-start.2 = ((bf16[16,2,5120]{2,1,0:T(2,128)(2,1)}), bf16[16,2,5120]{2,1,0:T(2,128)(2,1)S(1)}, u32[]{:S(2)}, u32[]{:S(2)}) async-start(bf16[16,2,5120]{2,1,0:T(2,128)(2,1)} %reshape.91), calls=%async_computation.2 | async-start | bytes 655360 | tf_op jit(solution)/shard_map/all_to_all | solution.py:83
  263.6 59.9 %all-gather.5.cloned.1.call-done = bf16[128,5120]{0,1:T(8,128)(2,1)} async-done(((bf16[128,160]{0,1:T(8,128)(2,1)}), bf16[128,5120]{0,1:T(8,128)(2,1)}) %all-gather.5.cloned.1.call-update) | async-done | bytes 1310736 | tf_op jit(solution)/shard_map/all_gather | solution.py:51
  323.6 1.8 fusion.21
  325.7 0.8 tile.2
  326.5 5.9 %all-to-all-start = ((bf16[128,32,48]{0,2,1:T(8,128)(2,1)}), bf16[128,32,48]{0,2,1:T(8,128)(2,1)S(1)}, u32[]{:S(2)}, u32[]{:S(2)}) async-start(bf16[128,32,48]{0,2,1:T(8,128)(2,1)} %tile.2), calls=%async_computation | async-start | bytes 786432 | tf_op jit(solution)/shard_map/all_to_all | solution.py:71
  332.6 2.7 convolution_bitcast_fusion
  335.3 0.9 reshape.92
  336.4 1.1 copy-done.5
  337.5 1.1 convolution_bitcast_fusion.1
  338.6 4.1 all-to-all-done
  343.3 135.9 %all-gather = bf16[512,1,640]{2,1,0:T(2,128)(2,1)S(1)} all-gather(bf16[1,1,640]{2,1,0:T(2,128)(2,1)S(1)} %reshape.83), channel_id=1, replica_groups=mesh['expert'=16,'tensor'=32] {'expert','tensor'}, dimensions={0}, use_global_device_ids=true | all-gather | bytes 656640 | tf_op jit(solution)/shard_map/all_gather | solution.py:91
  479.2 4.0 reduce
  483.2 0.7 reshape.81
  484.1 1.7 reshape.82
  485.8 0.7 exponential_reduce_fusion
  486.5 96.8 %all-reduce = (f32[64]{0:T(128)S(1)}, f32[64]{0:T(128)S(1)}) all-reduce(f32[64]{0:T(128)S(1)} %get-tuple-element.3, f32[64]{0:T(128)S(1)} %get-tuple-element.2), channel_id=1, replica_groups=mesh['expert'=16,'tensor'=32] {'expert','tensor'}, use_global_device_ids=true, to_apply=%region_4.5 | all-reduce | flops 128 | bytes 1024 | tf_op jit(solution)/shard_map/psum | solution.py:102
  583.4 0.5 log_subtract_fusion
  (48 shorter events, 3.0 us)
Async XLA Ops:
  7.2 478.7 %copy-start = (bf16[128,5120]{1,0:T(8,128)(2,1)S(1)}, bf16[128,5120]{1,0:T(8,128)(2,1)}, u32[]{:S(2)}) copy-start(bf16[128,5120]{1,0:T(8,128)(2,1)} %param.20) | copy-start | bytes 3932164
  7.2 145.9 %all-gather.7.cloned.1.call-start = ((), (), s32[]{:S(2)}) async-start(), calls=%async_computation.4 | async-start | bytes 10813440 | tf_op jit(solution)/shard_map/all_gather | solution.py:50
  8.4 3.8 copy-start.10
  12.6 140.5 %copy-start.3 = (bf16[1,48,5120]{2,1,0:T(8,128)(2,1)S(1)}, bf16[1,48,5120]{2,1,0:T(8,128)(2,1)}, u32[]{:S(2)}) copy-start(bf16[1,48,5120]{2,1,0:T(8,128)(2,1)} %param.14) | copy-start | bytes 1474564
  42.6 116.5 %copy-start.4 = (bf16[1,48,5120]{2,1,0:T(8,128)(2,1)S(1)}, bf16[1,48,5120]{2,1,0:T(8,128)(2,1)}, u32[]{:S(2)}) copy-start(bf16[1,48,5120]{2,1,0:T(8,128)(2,1)} %param.15) | copy-start | bytes 1474564
  42.6 199.7 %all-gather.9.cloned.1.call-start = ((), (), s32[]{:S(2)}) async-start(), calls=%async_computation.5 | async-start | bytes 3244032 | tf_op jit(solution)/shard_map/all_gather | solution.py:76
  153.1 7.0 %copy-start.1 = (bf16[1024,5120]{0,1:T(8,128)(2,1)S(1)}, bf16[1024,5120]{0,1:T(8,128)(2,1)}, u32[]{:S(2)}) copy-start(bf16[1024,5120]{0,1:T(8,128)(2,1)} %all-gather.7.cloned.1.call-done) | copy-start | bytes 31457284
  160.0 82.3 %copy-start.8 = (bf16[1,1536,160]{1,2,0:T(8,128)(2,1)S(1)}, bf16[1,1536,160]{1,2,0:T(8,128)(2,1)}, u32[]{:S(2)}) copy-start(bf16[1,1536,160]{1,2,0:T(8,128)(2,1)} %param.16) | copy-start | bytes 1474564
  162.7 160.9 %all-gather.5.cloned.1.call-start = ((), (), s32[]{:S(2)}) async-start(), calls=%async_computation.3 | async-start | bytes 1351680 | tf_op jit(solution)/shard_map/all_gather | solution.py:51
  250.3 73.2 %copy-start.6 = (bf16[48,5120]{1,0:T(8,128)(2,1)S(1)}, bf16[48,5120]{1,0:T(8,128)(2,1)}, u32[]{:S(2)}) copy-start(bf16[48,5120]{1,0:T(8,128)(2,1)} %param.17) | copy-start | bytes 1474564
  251.9 73.5 %copy-start.7 = (bf16[48,5120]{1,0:T(8,128)(2,1)S(1)}, bf16[48,5120]{1,0:T(8,128)(2,1)}, u32[]{:S(2)}) copy-start(bf16[48,5120]{1,0:T(8,128)(2,1)} %param.18) | copy-start | bytes 1474564
  251.9 73.9 %all-to-all-start.2 = ((bf16[16,2,5120]{2,1,0:T(2,128)(2,1)}), bf16[16,2,5120]{2,1,0:T(2,128)(2,1)S(1)}, u32[]{:S(2)}, u32[]{:S(2)}) async-start(bf16[16,2,5120]{2,1,0:T(2,128)(2,1)} %reshape.91), calls=%async_computation.2 | async-start | bytes 655360 | tf_op jit(solution)/shard_map/all_to_all | solution.py:83
  323.6 1.8 copy-start.2
  325.3 7.1 %copy-start.13 = (f32[128,6]{0,1:T(8,128)S(1)}, f32[128,6]{0,1:T(8,128)}, u32[]{:S(2)}) copy-start(f32[128,6]{0,1:T(8,128)} %param.13) | copy-start | bytes 9220
  326.5 16.2 %all-to-all-start = ((bf16[128,32,48]{0,2,1:T(8,128)(2,1)}), bf16[128,32,48]{0,2,1:T(8,128)(2,1)S(1)}, u32[]{:S(2)}, u32[]{:S(2)}) async-start(bf16[128,32,48]{0,2,1:T(8,128)(2,1)} %tile.2), calls=%async_computation | async-start | bytes 786432 | tf_op jit(solution)/shard_map/all_to_all | solution.py:71
  336.2 1.2 copy-start.5
  336.2 6.5 %copy-start.9 = (bf16[1536,160]{0,1:T(8,128)(2,1)S(1)}, bf16[1536,160]{0,1:T(8,128)(2,1)}, u32[]{:S(2)}) copy-start(bf16[1536,160]{0,1:T(8,128)(2,1)} %param.19) | copy-start | bytes 1474564
  336.3 6.4 %copy-start.11 = (bf16[128,160]{0,1:T(8,128)(2,1)S(1)}, bf16[128,160]{0,1:T(8,128)(2,1)}, u32[]{:S(2)}) copy-start(bf16[128,160]{0,1:T(8,128)(2,1)} %param.11) | copy-start | bytes 122884
  343.0 140.2 %copy-start.12 = (bf16[128,160]{0,1:T(8,128)(2,1)}, bf16[128,160]{0,1:T(8,128)(2,1)S(1)}, u32[]{:S(2)}) copy-start(bf16[128,160]{0,1:T(8,128)(2,1)S(1)} %fusion.4) | copy-start | bytes 122884
  484.1 1.7 copy-start.14
Sparse Core Ops, SparseCore 0:
  42.7 110.3 all-gather.6
  162.8 79.4 all-gather.8
  245.5 78.0 all-gather.4
